TPU v7x, 32 devices: a whole 2x2x4 slice. The times are simulated.
32 devices in a mesh: parts: 2 (over x), xline: 16 (over z, y, core).
Axes of the slice: x: 2, y: 2, z: 4, core: 2. Of those that a mesh axis runs over, the one named last changes fastest.
Arguments:
- gathers: bfloat16 [4, 96, 96, 256], P('parts', 'xline'), parts along dimension 0, may hold values from -6 to 6
- time_steps: float32 [2], replicated, may hold values from 0.3 to 0.8
- radon_op: bfloat16 [32, 2, 96, 96], P('xline'), may hold values from -0.4375 to 0.4375
Outputs:
- conditioned: bfloat16 [4, 96, 96, 256], P('parts', 'xline'), parts along dimension 0
There are 2 independent parts, one for each index of `parts`. A program takes and returns all parts, laid end to end along the dimension named above; an argument that names none is the same for every part. Nothing has to cross between parts.
All inputs are finite; a program needn't handle non-finite values.
Results may differ from a plain program's by a relative error of at most 0.0072.
Values may be sent and summed in bfloat16 or wider, within the bound.
No kernel may reach another device: no remote copies, remote signals or barrier semaphores. Data moves between devices by JAX's collectives and lax.ppermute only.
A program may use at most 128 MiB of HBM per device.

v0:
```python
import math
import jax
import jax.numpy as jnp
from jax import lax
from jax.sharding import PartitionSpec as P


def diff_depth(field):
    padded = jnp.pad(field, ((0, 0), (0, 0), (0, 0), (1, 1)))
    return 0.5 * (padded[..., 2:] - padded[..., :-2])


def box_depth(field):
    padded = jnp.pad(field, ((0, 0), (0, 0), (0, 0), (1, 1)))
    return (padded[..., :-2] + padded[..., 1:-1] + padded[..., 2:]) / 3.0


def diff_cross(field):
    return 0.5 * (field[:, 2:] - field[:, :-2])


def box_cross(field):
    return (field[:, :-2] + field[:, 1:-1] + field[:, 2:]) / 3.0


def diffuse(extended, tau_value, columns, total):
    inside = ((columns >= 0) & (columns < total)).astype(jnp.float32)[None, :, None, None]
    grad_cross = diff_cross(extended) * inside[:, 1:-1]
    grad_depth = diff_depth(extended[:, 1:-1]) * inside[:, 1:-1]
    tensor_xx = box_cross(box_depth(grad_cross * grad_cross)) * inside[:, 2:-2]
    tensor_xz = box_cross(box_depth(grad_cross * grad_depth)) * inside[:, 2:-2]
    tensor_zz = box_cross(box_depth(grad_depth * grad_depth)) * inside[:, 2:-2]
    norm_term = 1.0 + tensor_xx + tensor_zz
    inner_x = grad_cross[:, 1:-1]
    inner_z = grad_depth[:, 1:-1]
    flux_cross = inner_x - (tensor_xx * inner_x + tensor_xz * inner_z) / norm_term
    flux_depth = inner_z - (tensor_xz * inner_x + tensor_zz * inner_z) / norm_term
    change = diff_cross(flux_cross) + diff_depth(flux_depth[:, 1:-1])
    return (extended[:, 3:-3] + tau_value * change) * inside[:, 3:-3]


def forward_table(depth, bins):
    zeds = jnp.arange(depth, dtype=jnp.int32)[:, None]
    freqs = jnp.arange(bins, dtype=jnp.int32)[None, :]
    phase = (zeds * freqs % depth).astype(jnp.float32) * (2.0 * math.pi / depth)
    return jnp.concatenate([jnp.cos(phase), -jnp.sin(phase)], axis=1).astype(jnp.bfloat16)


def inverse_table(depth, bins):
    freqs = jnp.arange(bins, dtype=jnp.int32)[:, None]
    zeds = jnp.arange(depth, dtype=jnp.int32)[None, :]
    phase = (zeds * freqs % depth).astype(jnp.float32) * (2.0 * math.pi / depth)
    weight = jnp.where(freqs == 0, 1.0, 2.0).astype(jnp.float32) / depth
    return jnp.concatenate([weight * jnp.cos(phase), -weight * jnp.sin(phase)], axis=0).astype(
        jnp.bfloat16
    )


def complex_mats(operators):
    real_row = jnp.stack([operators[:, 0], -operators[:, 1]], axis=1)
    imag_row = jnp.stack([operators[:, 1], operators[:, 0]], axis=1)
    return jnp.stack([real_row, imag_row], axis=1)


def per_device(gathers, time_steps, radon_op):
    inlines, lines, offsets, depth = gathers.shape
    devices = lax.axis_size("xline")
    total = lines * devices
    bins = radon_op.shape[0] * devices
    steps_count = time_steps.shape[0]
    traces = jnp.transpose(gathers, (0, 2, 1, 3)).reshape(inlines * offsets, lines, depth)
    local_rows = lax.all_to_all(traces, "xline", split_axis=0, concat_axis=1, tiled=True)
    pair_rows = local_rows.shape[0]
    field = local_rows.astype(jnp.float32).reshape(pair_rows, total, 1, depth)
    columns = jnp.arange(-3, total + 3, dtype=jnp.int32)
    for number in range(steps_count):
        extended = jnp.pad(field, ((0, 0), (3, 3), (0, 0), (0, 0)))
        field = diffuse(extended, time_steps[number], columns, total)
    smooth = field.astype(jnp.bfloat16)
    spectrum = jnp.dot(
        smooth.reshape(-1, depth), forward_table(depth, bins), preferred_element_type=jnp.float32
    )
    spectrum = spectrum.astype(jnp.bfloat16).reshape(pair_rows, total, 2, bins)
    by_bins = lax.all_to_all(spectrum, "xline", split_axis=3, concat_axis=0, tiled=True)
    by_bins = by_bins.reshape(inlines, offsets, total, 2, radon_op.shape[0])
    mats = complex_mats(radon_op)
    done = jnp.einsum("ioxrf,fqrpo->ipxqf", by_bins, mats, preferred_element_type=jnp.float32)
    done = done.astype(jnp.bfloat16)
    back = lax.all_to_all(done, "xline", split_axis=2, concat_axis=4, tiled=True)
    filtered = jnp.transpose(back, (0, 2, 1, 3, 4))
    result = jnp.dot(
        filtered.reshape(-1, 2 * bins),
        inverse_table(depth, bins),
        preferred_element_type=jnp.float32,
    )
    return result.astype(jnp.bfloat16).reshape(inlines, lines, offsets, depth)


def solution(mesh):
    return jax.shard_map(
        per_device,
        mesh=mesh,
        in_specs=(P("parts", "xline", None, None), P(), P("xline", None, None, None)),
        out_specs=P("parts", "xline", None, None),
        check_vma=False,
    )
```

profile of v0, /device:TPU:0, one launch (start us, length us, event | category | flops | bytes accessed | tf_op | source)
XLA Modules:
  0.0 80.3 jit_solution(15486866586063491887)
XLA Ops:
  0.0 1.1 %copy.34 = bf16[2,6,96,256]{3,2,0,1:T(8,128)(2,1)S(1)} copy(bf16[2,6,96,256]{3,2,1,0:T(8,128)(2,1)} %param.3) | data formatting | bytes 1179648 | tf_op args[0]
  1.1 1.2 %copy.35 = bf16[192,6,256]{2,1,0:T(8,128)(2,1)} copy(bf16[192,6,256]{2,0,1:T(8,128)(2,1)S(1)} %bitcast.56) | data formatting | bytes 1179648 | tf_op jit(solution)/shard_map/reshape | solution.py:71
  2.3 7.4 %all-to-all-start = ((bf16[192,6,256]{2,1,0:T(8,128)(2,1)}), bf16[192,6,256]{2,1,0:T(8,128)(2,1)S(1)}, u32[]{:S(2)}, u32[]{:S(2)}) async-start(bf16[192,6,256]{2,1,0:T(8,128)(2,1)} %copy.35), calls=%async_computation | async-start | bytes 1572864 | tf_op jit(solution)/shard_map/all_to_all | solution.py:72
  9.8 0.6 fusion.81
  12.0 16.4 %all-to-all-done = bf16[192,6,256]{2,1,0:T(8,128)(2,1)S(1)} async-done(((bf16[192,6,256]{2,1,0:T(8,128)(2,1)}), bf16[192,6,256]{2,1,0:T(8,128)(2,1)S(1)}, u32[]{:S(2)}, u32[]{:S(2)}) %all-to-all-start) | async-done | bytes 589856 | tf_op jit(solution)/shard_map/all_to_all | solution.py:72
  28.7 0.7 copy.37
  29.7 0.8 fusion.79
  30.8 0.7 fusion.10
  31.6 1.4 %fusion.2 = (f32[12,100,1,256]{3,1,0,2:T(8,128)S(1)}, f32[12,100,1,256]{3,1,0,2:T(8,128)S(1)}) fusion(f32[12,100,1,256]{3,1,0,2:T(8,128)S(1)} %mul.293, f32[12,100,1,256]{3,1,0,2:T(8,128)S(1)} %get-tuple-element.16), kind=kLoop, calls=%fused_computation.24 | loop fusion | flops 1843200 | bytes 4915200 | tf_op jit(solution)/shard_map/div | solution.py:15
  33.0 2.9 %divide_subtract_fusion.1 = (f32[12,98,1,256]{3,1,0,2:T(8,128)S(1)}, f32[12,98,1,256]{3,1,0,2:T(8,128)}, f32[12,98,1,256]{3,1,0,2:T(8,128)S(1)}, f32[12,98,1,256...) fusion(f32[12,100,1,256]{3,1,0,2:T(8,128)S(1)} %get-tuple-element.18, ...), kind=kLoop, calls=%fused_computation.65 | loop fusion | flops 4816896 | bytes 20472200 | tf_op jit(solution)/shard_map/sub | solution.py:36
  36.0 1.1 %copy-done.2 = f32[12,98,1,256]{3,1,0,2:T(8,128)S(1)} copy-done((f32[12,98,1,256]{3,1,0,2:T(8,128)S(1)}, f32[12,98,1,256]{3,1,0,2:T(8,128)}, u32[]{:S(2)}) %copy-start.2) | copy-done | bytes 1204248
  37.1 0.4 copy-done.3
  37.5 0.4 copy-done.4
  37.9 0.7 fusion.41
  38.6 0.7 fusion.32
  39.5 0.8 fusion.74
  40.4 0.7 fusion.13
  41.3 0.7 fusion.21
  42.1 0.7 fusion.18
  42.8 3.0 %divide_subtract_fusion = (f32[12,98,1,256]{3,1,0,2:T(8,128)S(1)}, f32[12,98,1,256]{3,1,0,2:T(8,128)S(1)}, f32[12,98,1,256]{3,1,0,2:T(8,128)S(1)}, f32[12,98,1,2...) fusion(f32[12,100,1,256]{3,1,0,2:T(8,128)S(1)} %get-tuple-element.11, ...), kind=kLoop, calls=%fused_computation.62 | loop fusion | flops 4816896 | bytes 20472200 | tf_op jit(solution)/shard_map/sub | solution.py:36
  46.0 1.1 %copy-done = f32[12,98,1,256]{3,1,0,2:T(8,128)S(1)} copy-done((f32[12,98,1,256]{3,1,0,2:T(8,128)S(1)}, f32[12,98,1,256]{3,1,0,2:T(8,128)}, u32[]{:S(2)}) %copy-start) | copy-done | bytes 1204248
  47.1 0.4 copy-done.1
  47.5 0.7 fusion.39
  48.3 0.7 fusion.38
  49.3 0.3 reshape.81
  49.6 0.9 %copy.38 = bf16[12,96,2,32]{1,2,0,3:T(2,128)(2,1)} copy(bf16[12,96,2,32]{1,0,3,2:T(8,128)(2,1)S(1)} %reshape.81) | data formatting | bytes 294912 | tf_op jit(solution)/shard_map/reshape | solution.py:83
  50.5 5.4 %all-to-all-start.1 = ((bf16[12,96,2,32]{1,2,0,3:T(2,128)(2,1)}), bf16[12,96,2,32]{1,2,0,3:T(2,128)(2,1)S(1)}, u32[]{:S(2)}, u32[]{:S(2)}) async-start(bf16[12,96,2,32]{1,2,0,3:T(2,128)(2,1)} %copy.38), calls=%async_computation.1 | async-start | bytes 393216 | tf_op jit(solution)/shard_map/all_to_all | solution.py:84
  56.0 8.9 %all-to-all-done.1 = bf16[12,96,2,32]{1,2,0,3:T(2,128)(2,1)S(1)} async-done(((bf16[12,96,2,32]{1,2,0,3:T(2,128)(2,1)}), bf16[12,96,2,32]{1,2,0,3:T(2,128)(2,1)S(1)}, u32[]{:S(2)}, u32[]{:S(2)}) %all-to-all-start.1) | async-done | bytes 147488 | tf_op jit(solution)/shard_map/all_to_all | solution.py:84
  65.3 0.8 %copy.41 = bf16[2,96,96,2,2]{1,0,3,4,2:T(2,128)(2,1)} copy(bf16[2,96,96,2,2]{2,1,0,3,4:T(8,128)(2,1)S(1)} %fusion.44) | data formatting | bytes 294912 | tf_op jit(solution)/shard_map/convert_element_type | solution.py:88
  66.2 3.5 %all-to-all-start.2 = ((bf16[2,96,96,2,2]{1,0,3,4,2:T(2,128)(2,1)}), bf16[2,96,96,2,2]{1,0,3,4,2:T(2,128)(2,1)S(1)}, u32[]{:S(2)}, u32[]{:S(2)}) async-start(bf16[2,96,96,2,2]{1,0,3,4,2:T(2,128)(2,1)} %copy.41), calls=%async_computation.2 | async-start | bytes 393216 | tf_op jit(solution)/shard_map/all_to_all | solution.py:89
  69.9 8.8 %all-to-all-done.2 = bf16[2,96,96,2,2]{1,0,3,4,2:T(2,128)(2,1)S(1)} async-done(((bf16[2,96,96,2,2]{1,0,3,4,2:T(2,128)(2,1)}), bf16[2,96,96,2,2]{1,0,3,4,2:T(2,128)(2,1)S(1)}, u32[]{:S(2)}, u32[]{:S(2)}) %all-to-all-start.2) | async-done | bytes 147488 | tf_op jit(solution)/shard_map/all_to_all | solution.py:89
  79.2 1.2 %convolution_convert_fusion = bf16[1152,256]{1,0:T(8,128)(2,1)} fusion(bf16[1152,64]{0,1:T(8,128)(2,1)S(1)} %reshape.83, bf16[32,256]{1,0:T(8,128)(2,1)S(1)} %get-tuple-element.34, bf16[32,256]{1,0:T(8,128)(2,1)S(1)} %get-tuple-element.35), kind=kOutput, calls=%fused_computation | convolution fusion | flops 38109184 | bytes 770048 | tf_op jit(solution)/shard_map/dot_general | solution.py:91
  (36 shorter events, 3.5 us)
Async XLA Ops:
  1.1 8.7 %copy-start.6 = (f32[2]{0:T(128)S(1)}, f32[2]{0:T(128)}, u32[]{:S(2)}) copy-start(f32[2]{0:T(128)} %param.4) | copy-start | bytes 28
  2.3 26.1 %all-to-all-start = ((bf16[192,6,256]{2,1,0:T(8,128)(2,1)}), bf16[192,6,256]{2,1,0:T(8,128)(2,1)S(1)}, u32[]{:S(2)}, u32[]{:S(2)}) async-start(bf16[192,6,256]{2,1,0:T(8,128)(2,1)} %copy.35), calls=%async_computation | async-start | bytes 1572864 | tf_op jit(solution)/shard_map/all_to_all | solution.py:72
  35.8 1.3 %copy-start.2 = (f32[12,98,1,256]{3,1,0,2:T(8,128)S(1)}, f32[12,98,1,256]{3,1,0,2:T(8,128)}, u32[]{:S(2)}) copy-start(f32[12,98,1,256]{3,1,0,2:T(8,128)} %get-tuple-element.13) | copy-start | bytes 3612676
  35.8 1.7 %copy-start.3 = (f32[12,98,1,256]{3,1,0,2:T(8,128)S(1)}, f32[12,98,1,256]{3,1,0,2:T(8,128)}, u32[]{:S(2)}) copy-start(f32[12,98,1,256]{3,1,0,2:T(8,128)} %get-tuple-element.21) | copy-start | bytes 3612676
  35.8 2.1 %copy-start.4 = (f32[12,98,1,256]{3,1,0,2:T(8,128)S(1)}, f32[12,98,1,256]{3,1,0,2:T(8,128)}, u32[]{:S(2)}) copy-start(f32[12,98,1,256]{3,1,0,2:T(8,128)} %get-tuple-element.22) | copy-start | bytes 3612676
  45.8 1.3 %copy-start = (f32[12,98,1,256]{3,1,0,2:T(8,128)S(1)}, f32[12,98,1,256]{3,1,0,2:T(8,128)}, u32[]{:S(2)}) copy-start(f32[12,98,1,256]{3,1,0,2:T(8,128)} %get-tuple-element.19) | copy-start | bytes 3612676
  45.8 1.7 %copy-start.1 = (f32[12,98,1,256]{3,1,0,2:T(8,128)S(1)}, f32[12,98,1,256]{3,1,0,2:T(8,128)}, u32[]{:S(2)}) copy-start(f32[12,98,1,256]{3,1,0,2:T(8,128)} %get-tuple-element.20) | copy-start | bytes 3612676
  49.0 6.9 %copy-start.5 = (bf16[2,2,96,96]{3,2,1,0:T(8,128)(2,1)S(1)}, bf16[2,2,96,96]{3,2,1,0:T(8,128)(2,1)}, u32[]{:S(2)}) copy-start(bf16[2,2,96,96]{3,2,1,0:T(8,128)(2,1)} %param.5) | copy-start | bytes 221188
  50.5 14.3 %all-to-all-start.1 = ((bf16[12,96,2,32]{1,2,0,3:T(2,128)(2,1)}), bf16[12,96,2,32]{1,2,0,3:T(2,128)(2,1)S(1)}, u32[]{:S(2)}, u32[]{:S(2)}) async-start(bf16[12,96,2,32]{1,2,0,3:T(2,128)(2,1)} %copy.38), calls=%async_computation.1 | async-start | bytes 393216 | tf_op jit(solution)/shard_map/all_to_all | solution.py:84
  66.2 12.5 %all-to-all-start.2 = ((bf16[2,96,96,2,2]{1,0,3,4,2:T(2,128)(2,1)}), bf16[2,96,96,2,2]{1,0,3,4,2:T(2,128)(2,1)S(1)}, u32[]{:S(2)}, u32[]{:S(2)}) async-start(bf16[2,96,96,2,2]{1,0,3,4,2:T(2,128)(2,1)} %copy.41), calls=%async_computation.2 | async-start | bytes 393216 | tf_op jit(solution)/shard_map/all_to_all | solution.py:89
where the time goes:
time: 80.8 us; the launch traced here: 80.3 us
  waiting for transfers between devices  34 us (42%)
  starting transfers between devices  16.3 us (20%)
  other arithmetic  16.3 us (20%)
  local copies, waits for them, and re-layouts  10.4 us (13%)
  matrix products  1.73 us (2%)
  between operations  1.56 us (2%)
    all_to_all x1, waiting for transfers between devices, per_device(): lax.all_to_all(traces, 'xline', split_axis=0, concat_axis=1, tiled=True)  16.4 us
    all_to_all x1, waiting for transfers between devices, per_device(): lax.all_to_all(spectrum, 'xline', split_axis=3, concat_axis=0, tiled=True)  8.87 us
    all_to_all x1, waiting for transfers between devices, per_device(): lax.all_to_all(done, 'xline', split_axis=2, concat_axis=4, tiled=True)  8.76 us
    all_to_all x1, starting transfers between devices, per_device(): lax.all_to_all(traces, 'xline', split_axis=0, concat_axis=1, tiled=True)  7.41 us
    sub x2, other arithmetic, diffuse(): inner_x - (tensor_xx * inner_x + tensor_xz * inner_z) / norm_term  5.89 us
    all_to_all x1, starting transfers between devices, per_device(): lax.all_to_all(spectrum, 'xline', split_axis=3, concat_axis=0, tiled=True)  5.38 us
    unnamed x15, local copies, waits for them, and re-layouts  4.54 us
    div x5, other arithmetic, box_depth(): return (padded[..., :-2] + padded[..., 1:-1] + padded[..., 2:]) / 3.0  4.28 us
  transfers between devices with their start and end apart: 3, of which 3 were waited for; matrix products, arithmetic and copies ran while one was open for 1% of the time, Pallas kernels for 0%

commit v1 on v0

--- a/solution.py
+++ b/solution.py
@@ -3,6 +3,29 @@
 import jax.numpy as jnp
 from jax import lax
 from jax.sharding import PartitionSpec as P
+
+
+def in_blocks(shard, dim, size):
+    shape = shard.shape
+    tiles = shard.reshape(*shape[:dim], size, shape[dim] // size, *shape[dim + 1 :])
+    return jnp.moveaxis(tiles, dim, 0)
+
+
+def in_order(tiles, dim):
+    dims = list(tiles.shape[1:])
+    dims[dim] *= tiles.shape[0]
+    return jnp.moveaxis(tiles, 0, dim).reshape(dims)
+
+
+def swapped_with_each(value, axis, split_dim, concat_dim):
+    size, place = (lax.axis_size(axis), lax.axis_index(axis))
+    blocks = in_blocks(value, split_dim, size)
+    outs = [blocks[place]]
+    for step in range(1, size):
+        sent = blocks[place ^ step]
+        outs.append(lax.ppermute(sent, axis, [(i, i ^ step) for i in range(size)]))
+    blocks = jnp.stack(outs)[place ^ jnp.arange(size)]
+    return in_order(blocks, concat_dim)
 
 
 def diff_depth(field):
@@ -86,7 +109,7 @@
     mats = complex_mats(radon_op)
     done = jnp.einsum("ioxrf,fqrpo->ipxqf", by_bins, mats, preferred_element_type=jnp.float32)
     done = done.astype(jnp.bfloat16)
-    back = lax.all_to_all(done, "xline", split_axis=2, concat_axis=4, tiled=True)
+    back = swapped_with_each(done, "xline", 2, 4)
     filtered = jnp.transpose(back, (0, 2, 1, 3, 4))
     result = jnp.dot(
         filtered.reshape(-1, 2 * bins),

time: 80.8 us -> 92.9 us (1.15)
  starting transfers between devices: 16.3 us -> 33.9 us
  waiting for transfers between devices: 34 us -> 27.5 us
    ppermute x0 -> x15, starting transfers between devices: none -> 21.1 us  [swapped_with_each(): outs.append(lax.ppermute(sent, axis, [(i, i ^ step) for i in range(size)]))]
    all_to_all x1 -> x0, waiting for transfers between devices: 8.76 us -> none  [per_device(): lax.all_to_all(done, 'xline', split_axis=2, concat_axis=4, tiled=True)]
    all_to_all x1 -> x0, starting transfers between devices: 3.52 us -> none  [per_device(): lax.all_to_all(done, 'xline', split_axis=2, concat_axis=4, tiled=True)]
    ppermute x0 -> x15, waiting for transfers between devices: none -> 2.59 us  [swapped_with_each(): outs.append(lax.ppermute(sent, axis, [(i, i ^ step) for i in range(size)]))]
    gather x0 -> x1, local copies, waits for them, and re-layouts: none -> 0.94 us  [swapped_with_each(): blocks = jnp.stack(outs)[place ^ jnp.arange(size)]]
    unnamed x15 -> x30, local copies, waits for them, and re-layouts: 4.54 us -> 4.79 us
  transfers between devices with their start and end apart: 3 -> 17, of which waited for: 3 -> 4; matrix products, arithmetic and copies ran while one was open for 1% -> 2% of each run, Pallas kernels for 0% -> 0%
where the time goes in v1:
time: 92.9 us; the launch traced here: 92.5 us
  starting transfers between devices  33.9 us (36%)
  waiting for transfers between devices  27.5 us (30%)
  other arithmetic  16.4 us (18%)
  local copies, waits for them, and re-layouts  11.1 us (12%)
  between operations  1.8 us (2%)
  matrix products  1.73 us (2%)
    ppermute x15, starting transfers between devices, swapped_with_each(): outs.append(lax.ppermute(sent, axis, [(i, i ^ step) for i in range(size)]))  21.1 us
    all_to_all x1, waiting for transfers between devices, per_device(): lax.all_to_all(traces, 'xline', split_axis=0, concat_axis=1, tiled=True)  16.2 us
    all_to_all x1, waiting for transfers between devices, per_device(): lax.all_to_all(spectrum, 'xline', split_axis=3, concat_axis=0, tiled=True)  8.72 us
    all_to_all x1, starting transfers between devices, per_device(): lax.all_to_all(traces, 'xline', split_axis=0, concat_axis=1, tiled=True)  7.41 us
    sub x2, other arithmetic, diffuse(): inner_x - (tensor_xx * inner_x + tensor_xz * inner_z) / norm_term  5.9 us
    all_to_all x1, starting transfers between devices, per_device(): lax.all_to_all(spectrum, 'xline', split_axis=3, concat_axis=0, tiled=True)  5.38 us
    unnamed x30, local copies, waits for them, and re-layouts  4.79 us
    div x5, other arithmetic, box_depth(): return (padded[..., :-2] + padded[..., 1:-1] + padded[..., 2:]) / 3.0  4.28 us
  transfers between devices with their start and end apart: 17, of which 4 were waited for; matrix products, arithmetic and copies ran while one was open for 2% of the time, Pallas kernels for 0%

profile of v1, /device:TPU:0, one launch (start us, length us, event | category | flops | bytes accessed | tf_op | source)
XLA Modules:
  0.0 92.5 jit_solution(6184504206814267926)
XLA Ops:
  0.0 1.1 %copy.31 = bf16[2,6,96,256]{3,2,0,1:T(8,128)(2,1)S(1)} copy(bf16[2,6,96,256]{3,2,1,0:T(8,128)(2,1)} %param.3) | data formatting | bytes 1179648 | tf_op args[0]
  1.1 1.2 %copy.32 = bf16[192,6,256]{2,1,0:T(8,128)(2,1)} copy(bf16[192,6,256]{2,0,1:T(8,128)(2,1)S(1)} %bitcast.120) | data formatting | bytes 1179648 | tf_op jit(solution)/shard_map/reshape | solution.py:94
  2.4 7.4 %all-to-all-start = ((bf16[192,6,256]{2,1,0:T(8,128)(2,1)}), bf16[192,6,256]{2,1,0:T(8,128)(2,1)S(1)}, u32[]{:S(2)}, u32[]{:S(2)}) async-start(bf16[192,6,256]{2,1,0:T(8,128)(2,1)} %copy.32), calls=%async_computation | async-start | bytes 1572864 | tf_op jit(solution)/shard_map/all_to_all | solution.py:95
  12.3 16.2 %all-to-all-done = bf16[192,6,256]{2,1,0:T(8,128)(2,1)S(1)} async-done(((bf16[192,6,256]{2,1,0:T(8,128)(2,1)}), bf16[192,6,256]{2,1,0:T(8,128)(2,1)S(1)}, u32[]{:S(2)}, u32[]{:S(2)}) %all-to-all-start) | async-done | bytes 589856 | tf_op jit(solution)/shard_map/all_to_all | solution.py:95
  29.7 0.8 fusion.80
  31.6 1.4 %fusion.2 = (f32[12,100,1,256]{3,1,0,2:T(8,128)S(1)}, f32[12,100,1,256]{3,1,0,2:T(8,128)S(1)}) fusion(f32[12,100,1,256]{3,1,0,2:T(8,128)S(1)} %mul.293, f32[12,100,1,256]{3,1,0,2:T(8,128)S(1)} %get-tuple-element.16), kind=kLoop, calls=%fused_computation.25 | loop fusion | flops 1843200 | bytes 4915200 | tf_op jit(solution)/shard_map/div | solution.py:38
  33.0 2.9 %divide_subtract_fusion.1 = (f32[12,98,1,256]{3,1,0,2:T(8,128)S(1)}, f32[12,98,1,256]{3,1,0,2:T(8,128)}, f32[12,98,1,256]{3,1,0,2:T(8,128)S(1)}, f32[12,98,1,256...) fusion(f32[12,100,1,256]{3,1,0,2:T(8,128)S(1)} %get-tuple-element.18, ...), kind=kLoop, calls=%fused_computation.66 | loop fusion | flops 4816896 | bytes 20472200 | tf_op jit(solution)/shard_map/sub | solution.py:59
  36.0 1.1 %copy-done.2 = f32[12,98,1,256]{3,1,0,2:T(8,128)S(1)} copy-done((f32[12,98,1,256]{3,1,0,2:T(8,128)S(1)}, f32[12,98,1,256]{3,1,0,2:T(8,128)}, u32[]{:S(2)}) %copy-start.2) | copy-done | bytes 1204248
  37.9 0.7 fusion.41
  38.7 0.7 fusion.32
  39.5 0.8 fusion.75
  40.5 0.7 fusion.13
  42.8 3.0 %divide_subtract_fusion = (f32[12,98,1,256]{3,1,0,2:T(8,128)S(1)}, f32[12,98,1,256]{3,1,0,2:T(8,128)S(1)}, f32[12,98,1,256]{3,1,0,2:T(8,128)S(1)}, f32[12,98,1,2...) fusion(f32[12,100,1,256]{3,1,0,2:T(8,128)S(1)} %get-tuple-element.11, ...), kind=kLoop, calls=%fused_computation.63 | loop fusion | flops 4816896 | bytes 20472200 | tf_op jit(solution)/shard_map/sub | solution.py:59
  46.0 1.1 %copy-done = f32[12,98,1,256]{3,1,0,2:T(8,128)S(1)} copy-done((f32[12,98,1,256]{3,1,0,2:T(8,128)S(1)}, f32[12,98,1,256]{3,1,0,2:T(8,128)}, u32[]{:S(2)}) %copy-start) | copy-done | bytes 1204248
  47.5 0.7 fusion.39
  49.6 0.9 copy.35
  50.5 5.4 %all-to-all-start.1 = ((bf16[12,96,2,32]{1,2,0,3:T(2,128)(2,1)}), bf16[12,96,2,32]{1,2,0,3:T(2,128)(2,1)S(1)}, u32[]{:S(2)}, u32[]{:S(2)}) async-start(bf16[12,96,2,32]{1,2,0,3:T(2,128)(2,1)} %copy.35), calls=%async_computation.1 | async-start | bytes 393216 | tf_op jit(solution)/shard_map/all_to_all | solution.py:107
  56.1 8.7 %all-to-all-done.1 = bf16[12,96,2,32]{1,2,0,3:T(2,128)(2,1)S(1)} async-done(((bf16[12,96,2,32]{1,2,0,3:T(2,128)(2,1)}), bf16[12,96,2,32]{1,2,0,3:T(2,128)(2,1)S(1)}, u32[]{:S(2)}, u32[]{:S(2)}) %all-to-all-start.1) | async-done | bytes 147488 | tf_op jit(solution)/shard_map/all_to_all | solution.py:107
  66.1 1.6 %collective-permute-start.2 = (bf16[2,96,6,2,2]{1,4,3,2,0:T(2,128)(2,1)S(1)}, bf16[2,96,6,2,2]{1,4,3,2,0:T(2,128)(2,1)S(1)}, u32[]{:S(2)}, u32[]{:S(2)}) collective-permute-start(bf16[2,96,6,2,2]{1,4,3,2,0:T(2,128)(2,1)S(1)} %get-tuple-element.35), channel_id=1, source_target_pairs={{0,3},{1,2},{2,1},{3,0},{4,7},{5,6},{6,5},{7,4},{8,11},{9,10},{10,... | collective-permute-start | bytes 27656 | tf_op jit(solution)/shard_map/ppermute | solution.py:26
  67.7 1.7 %collective-permute-start.4 = (bf16[2,96,6,2,2]{1,4,3,2,0:T(2,128)(2,1)S(1)}, bf16[2,96,6,2,2]{1,4,3,2,0:T(2,128)(2,1)S(1)}, u32[]{:S(2)}, u32[]{:S(2)}) collective-permute-start(bf16[2,96,6,2,2]{1,4,3,2,0:T(2,128)(2,1)S(1)} %get-tuple-element.33), channel_id=1, source_target_pairs={{0,5},{1,4},{2,7},{3,6},{4,1},{5,0},{6,3},{7,2},{8,13},{9,12},{10,... | collective-permute-start | bytes 27656 | tf_op jit(solution)/shard_map/ppermute | solution.py:26
  69.9 2.3 %collective-permute-start.6 = (bf16[2,96,6,2,2]{1,4,3,2,0:T(2,128)(2,1)S(1)}, bf16[2,96,6,2,2]{1,4,3,2,0:T(2,128)(2,1)S(1)}, u32[]{:S(2)}, u32[]{:S(2)}) collective-permute-start(bf16[2,96,6,2,2]{1,4,3,2,0:T(2,128)(2,1)S(1)} %get-tuple-element.31), channel_id=1, source_target_pairs={{0,7},{1,6},{2,5},{3,4},{4,3},{5,2},{6,1},{7,0},{8,15},{9,14},{10,... | collective-permute-start | bytes 27656 | tf_op jit(solution)/shard_map/ppermute | solution.py:26
  72.2 0.8 collective-permute-start.7
  73.0 1.9 %collective-permute-start.8 = (bf16[2,96,6,2,2]{1,4,3,2,0:T(2,128)(2,1)S(1)}, bf16[2,96,6,2,2]{1,4,3,2,0:T(2,128)(2,1)S(1)}, u32[]{:S(2)}, u32[]{:S(2)}) collective-permute-start(bf16[2,96,6,2,2]{1,4,3,2,0:T(2,128)(2,1)S(1)} %get-tuple-element.29), channel_id=1, source_target_pairs={{0,9},{1,8},{2,11},{3,10},{4,13},{5,12},{6,15},{7,14},{8,1},{9,0},... | collective-permute-start | bytes 27656 | tf_op jit(solution)/shard_map/ppermute | solution.py:26
  75.4 3.3 %collective-permute-start.10 = (bf16[2,96,6,2,2]{1,4,3,2,0:T(2,128)(2,1)S(1)}, bf16[2,96,6,2,2]{1,4,3,2,0:T(2,128)(2,1)S(1)}, u32[]{:S(2)}, u32[]{:S(2)}) collective-permute-start(bf16[2,96,6,2,2]{1,4,3,2,0:T(2,128)(2,1)S(1)} %get-tuple-element.27), channel_id=1, source_target_pairs={{0,11},{1,10},{2,9},{3,8},{4,15},{5,14},{6,13},{7,12},{8,3},{9,2},... | collective-permute-start | bytes 27656 | tf_op jit(solution)/shard_map/ppermute | solution.py:26
  78.8 0.9 collective-permute-start.11
  79.7 2.7 %collective-permute-start.12 = (bf16[2,96,6,2,2]{1,4,3,2,0:T(2,128)(2,1)S(1)}, bf16[2,96,6,2,2]{1,4,3,2,0:T(2,128)(2,1)S(1)}, u32[]{:S(2)}, u32[]{:S(2)}) collective-permute-start(bf16[2,96,6,2,2]{1,4,3,2,0:T(2,128)(2,1)S(1)} %get-tuple-element.25), channel_id=1, source_target_pairs={{0,13},{1,12},{2,15},{3,14},{4,9},{5,8},{6,11},{7,10},{8,5},{9,4},... | collective-permute-start | bytes 27656 | tf_op jit(solution)/shard_map/ppermute | solution.py:26
  82.4 1.5 %collective-permute-start.13 = (bf16[2,96,6,2,2]{1,4,3,2,0:T(2,128)(2,1)S(1)}, bf16[2,96,6,2,2]{1,4,3,2,0:T(2,128)(2,1)S(1)}, u32[]{:S(2)}, u32[]{:S(2)}) collective-permute-start(bf16[2,96,6,2,2]{1,4,3,2,0:T(2,128)(2,1)S(1)} %get-tuple-element.24), channel_id=1, source_target_pairs={{0,14},{1,15},{2,12},{3,13},{4,10},{5,11},{6,8},{7,9},{8,6},{9,7},... | collective-permute-start | bytes 27656 | tf_op jit(solution)/shard_map/ppermute | solution.py:26
  83.9 3.2 %collective-permute-start.14 = (bf16[2,96,6,2,2]{1,4,3,2,0:T(2,128)(2,1)S(1)}, bf16[2,96,6,2,2]{1,4,3,2,0:T(2,128)(2,1)S(1)}, u32[]{:S(2)}, u32[]{:S(2)}) collective-permute-start(bf16[2,96,6,2,2]{1,4,3,2,0:T(2,128)(2,1)S(1)} %get-tuple-element.23), channel_id=1, source_target_pairs={{0,15},{1,14},{2,13},{3,12},{4,11},{5,10},{6,9},{7,8},{8,7},{9,6},... | collective-permute-start | bytes 27656 | tf_op jit(solution)/shard_map/ppermute | solution.py:26
  87.2 1.7 %collective-permute-done.13 = bf16[2,96,6,2,2]{1,4,3,2,0:T(2,128)(2,1)S(1)} collective-permute-done((bf16[2,96,6,2,2]{1,4,3,2,0:T(2,128)(2,1)S(1)}, bf16[2,96,6,2,2]{1,4,3,2,0:T(2,128)(2,1)S(1)}, u32[]{:S(2)}, u32[]{:S(2)}) %collective-permute-start.13) | collective-permute-done | bytes 9248 | tf_op jit(solution)/shard_map/ppermute | solution.py:26
  88.9 0.9 collective-permute-done.14
  89.8 0.9 %gather_fusion = bf16[16,2,96,6,2,2]{2,5,4,3,1,0:T(2,128)(2,1)S(1)} fusion(bf16[16,2,96,6,2,2]{2,5,4,3,1,0:T(2,128)(2,1)S(1)} %constant_dynamic-update-slice_fusion, s32[1024]{0:T(1024)S(1)} %pad_clamp_fusion), kind=kCustom, calls=%fused_computation | custom fusion | bytes 294976 | tf_op jit(solution)/shard_map/gather | solution.py:27
  91.3 1.2 %convolution_convert_fusion = bf16[1152,256]{1,0:T(8,128)(2,1)} fusion(bf16[1152,64]{0,1:T(8,128)(2,1)S(1)} %reshape.138, bf16[32,256]{1,0:T(8,128)(2,1)S(1)} %multiply_convert_fusion, bf16[32,256]{1,0:T(8,128)(2,1)S(1)} %multiply_convert_fusion.1), kind=kOutput, calls=%fused_computation.1 | convolution fusion | flops 38109184 | bytes 770048 | tf_op jit(solution)/shard_map/dot_general | solution.py:114
  (84 shorter events, 11.3 us)
Async XLA Ops:
  1.1 8.9 %copy-start.6 = (f32[2]{0:T(128)S(1)}, f32[2]{0:T(128)}, u32[]{:S(2)}) copy-start(f32[2]{0:T(128)} %param.4) | copy-start | bytes 28
  1.1 10.7 %copy-start.5 = (bf16[2,2,96,96]{3,2,1,0:T(8,128)(2,1)S(1)}, bf16[2,2,96,96]{3,2,1,0:T(8,128)(2,1)}, u32[]{:S(2)}) copy-start(bf16[2,2,96,96]{3,2,1,0:T(8,128)(2,1)} %param.5) | copy-start | bytes 221188
  2.4 26.1 %all-to-all-start = ((bf16[192,6,256]{2,1,0:T(8,128)(2,1)}), bf16[192,6,256]{2,1,0:T(8,128)(2,1)S(1)}, u32[]{:S(2)}, u32[]{:S(2)}) async-start(bf16[192,6,256]{2,1,0:T(8,128)(2,1)} %copy.32), calls=%async_computation | async-start | bytes 1572864 | tf_op jit(solution)/shard_map/all_to_all | solution.py:95
  35.8 1.3 %copy-start.2 = (f32[12,98,1,256]{3,1,0,2:T(8,128)S(1)}, f32[12,98,1,256]{3,1,0,2:T(8,128)}, u32[]{:S(2)}) copy-start(f32[12,98,1,256]{3,1,0,2:T(8,128)} %get-tuple-element.13) | copy-start | bytes 3612676
  35.8 1.7 %copy-start.3 = (f32[12,98,1,256]{3,1,0,2:T(8,128)S(1)}, f32[12,98,1,256]{3,1,0,2:T(8,128)}, u32[]{:S(2)}) copy-start(f32[12,98,1,256]{3,1,0,2:T(8,128)} %get-tuple-element.21) | copy-start | bytes 3612676
  35.8 2.1 %copy-start.4 = (f32[12,98,1,256]{3,1,0,2:T(8,128)S(1)}, f32[12,98,1,256]{3,1,0,2:T(8,128)}, u32[]{:S(2)}) copy-start(f32[12,98,1,256]{3,1,0,2:T(8,128)} %get-tuple-element.22) | copy-start | bytes 3612676
  45.9 1.3 %copy-start = (f32[12,98,1,256]{3,1,0,2:T(8,128)S(1)}, f32[12,98,1,256]{3,1,0,2:T(8,128)}, u32[]{:S(2)}) copy-start(f32[12,98,1,256]{3,1,0,2:T(8,128)} %get-tuple-element.19) | copy-start | bytes 3612676
  45.9 1.7 %copy-start.1 = (f32[12,98,1,256]{3,1,0,2:T(8,128)S(1)}, f32[12,98,1,256]{3,1,0,2:T(8,128)}, u32[]{:S(2)}) copy-start(f32[12,98,1,256]{3,1,0,2:T(8,128)} %get-tuple-element.20) | copy-start | bytes 3612676
  50.5 14.3 %all-to-all-start.1 = ((bf16[12,96,2,32]{1,2,0,3:T(2,128)(2,1)}), bf16[12,96,2,32]{1,2,0,3:T(2,128)(2,1)S(1)}, u32[]{:S(2)}, u32[]{:S(2)}) async-start(bf16[12,96,2,32]{1,2,0,3:T(2,128)(2,1)} %copy.35), calls=%async_computation.1 | async-start | bytes 393216 | tf_op jit(solution)/shard_map/all_to_all | solution.py:107
  65.7 3.7 %collective-permute-start = (bf16[2,96,6,2,2]{1,4,3,2,0:T(2,128)(2,1)S(1)}, bf16[2,96,6,2,2]{1,4,3,2,0:T(2,128)(2,1)S(1)}, u32[]{:S(2)}, u32[]{:S(2)}) collective-permute-start(bf16[2,96,6,2,2]{1,4,3,2,0:T(2,128)(2,1)S(1)} %get-tuple-element.37), channel_id=1, source_target_pairs={{0,1},{1,0},{2,3},{3,2},{4,5},{5,4},{6,7},{7,6},{8,9},{9,8},{10,11... | collective-permute-start | bytes 27656 | tf_op jit(solution)/shard_map/ppermute | solution.py:26
  65.8 4.1 %collective-permute-start.1 = (bf16[2,96,6,2,2]{1,4,3,2,0:T(2,128)(2,1)S(1)}, bf16[2,96,6,2,2]{1,4,3,2,0:T(2,128)(2,1)S(1)}, u32[]{:S(2)}, u32[]{:S(2)}) collective-permute-start(bf16[2,96,6,2,2]{1,4,3,2,0:T(2,128)(2,1)S(1)} %get-tuple-element.36), channel_id=1, source_target_pairs={{0,2},{1,3},{2,0},{3,1},{4,6},{5,7},{6,4},{7,5},{8,10},{9,11},{10,... | collective-permute-start | bytes 27656 | tf_op jit(solution)/shard_map/ppermute | solution.py:26
  66.1 6.1 %collective-permute-start.2 = (bf16[2,96,6,2,2]{1,4,3,2,0:T(2,128)(2,1)S(1)}, bf16[2,96,6,2,2]{1,4,3,2,0:T(2,128)(2,1)S(1)}, u32[]{:S(2)}, u32[]{:S(2)}) collective-permute-start(bf16[2,96,6,2,2]{1,4,3,2,0:T(2,128)(2,1)S(1)} %get-tuple-element.35), channel_id=1, source_target_pairs={{0,3},{1,2},{2,1},{3,0},{4,7},{5,6},{6,5},{7,4},{8,11},{9,10},{10,... | collective-permute-start | bytes 27656 | tf_op jit(solution)/shard_map/ppermute | solution.py:26
  67.7 5.3 %collective-permute-start.3 = (bf16[2,96,6,2,2]{1,4,3,2,0:T(2,128)(2,1)S(1)}, bf16[2,96,6,2,2]{1,4,3,2,0:T(2,128)(2,1)S(1)}, u32[]{:S(2)}, u32[]{:S(2)}) collective-permute-start(bf16[2,96,6,2,2]{1,4,3,2,0:T(2,128)(2,1)S(1)} %get-tuple-element.34), channel_id=1, source_target_pairs={{0,4},{1,5},{2,6},{3,7},{4,0},{5,1},{6,2},{7,3},{8,12},{9,13},{10,... | collective-permute-start | bytes 27656 | tf_op jit(solution)/shard_map/ppermute | solution.py:26
  67.7 7.2 %collective-permute-start.4 = (bf16[2,96,6,2,2]{1,4,3,2,0:T(2,128)(2,1)S(1)}, bf16[2,96,6,2,2]{1,4,3,2,0:T(2,128)(2,1)S(1)}, u32[]{:S(2)}, u32[]{:S(2)}) collective-permute-start(bf16[2,96,6,2,2]{1,4,3,2,0:T(2,128)(2,1)S(1)} %get-tuple-element.33), channel_id=1, source_target_pairs={{0,5},{1,4},{2,7},{3,6},{4,1},{5,0},{6,3},{7,2},{8,13},{9,12},{10,... | collective-permute-start | bytes 27656 | tf_op jit(solution)/shard_map/ppermute | solution.py:26
  69.4 6.1 %collective-permute-start.5 = (bf16[2,96,6,2,2]{1,4,3,2,0:T(2,128)(2,1)S(1)}, bf16[2,96,6,2,2]{1,4,3,2,0:T(2,128)(2,1)S(1)}, u32[]{:S(2)}, u32[]{:S(2)}) collective-permute-start(bf16[2,96,6,2,2]{1,4,3,2,0:T(2,128)(2,1)S(1)} %get-tuple-element.32), channel_id=1, source_target_pairs={{0,6},{1,7},{2,4},{3,5},{4,2},{5,3},{6,0},{7,1},{8,14},{9,15},{10,... | collective-permute-start | bytes 27656 | tf_op jit(solution)/shard_map/ppermute | solution.py:26
  69.9 8.9 %collective-permute-start.6 = (bf16[2,96,6,2,2]{1,4,3,2,0:T(2,128)(2,1)S(1)}, bf16[2,96,6,2,2]{1,4,3,2,0:T(2,128)(2,1)S(1)}, u32[]{:S(2)}, u32[]{:S(2)}) collective-permute-start(bf16[2,96,6,2,2]{1,4,3,2,0:T(2,128)(2,1)S(1)} %get-tuple-element.31), channel_id=1, source_target_pairs={{0,7},{1,6},{2,5},{3,4},{4,3},{5,2},{6,1},{7,0},{8,15},{9,14},{10,... | collective-permute-start | bytes 27656 | tf_op jit(solution)/shard_map/ppermute | solution.py:26
  72.2 7.5 %collective-permute-start.7 = (bf16[2,96,6,2,2]{1,4,3,2,0:T(2,128)(2,1)S(1)}, bf16[2,96,6,2,2]{1,4,3,2,0:T(2,128)(2,1)S(1)}, u32[]{:S(2)}, u32[]{:S(2)}) collective-permute-start(bf16[2,96,6,2,2]{1,4,3,2,0:T(2,128)(2,1)S(1)} %get-tuple-element.30), channel_id=1, source_target_pairs={{0,8},{1,9},{2,10},{3,11},{4,12},{5,13},{6,14},{7,15},{8,0},{9,1},... | collective-permute-start | bytes 27656 | tf_op jit(solution)/shard_map/ppermute | solution.py:26
  73.0 9.4 %collective-permute-start.8 = (bf16[2,96,6,2,2]{1,4,3,2,0:T(2,128)(2,1)S(1)}, bf16[2,96,6,2,2]{1,4,3,2,0:T(2,128)(2,1)S(1)}, u32[]{:S(2)}, u32[]{:S(2)}) collective-permute-start(bf16[2,96,6,2,2]{1,4,3,2,0:T(2,128)(2,1)S(1)} %get-tuple-element.29), channel_id=1, source_target_pairs={{0,9},{1,8},{2,11},{3,10},{4,13},{5,12},{6,15},{7,14},{8,1},{9,0},... | collective-permute-start | bytes 27656 | tf_op jit(solution)/shard_map/ppermute | solution.py:26
  75.0 8.9 %collective-permute-start.9 = (bf16[2,96,6,2,2]{1,4,3,2,0:T(2,128)(2,1)S(1)}, bf16[2,96,6,2,2]{1,4,3,2,0:T(2,128)(2,1)S(1)}, u32[]{:S(2)}, u32[]{:S(2)}) collective-permute-start(bf16[2,96,6,2,2]{1,4,3,2,0:T(2,128)(2,1)S(1)} %get-tuple-element.28), channel_id=1, source_target_pairs={{0,10},{1,11},{2,8},{3,9},{4,14},{5,15},{6,12},{7,13},{8,2},{9,3},... | collective-permute-start | bytes 27656 | tf_op jit(solution)/shard_map/ppermute | solution.py:26
  75.4 11.7 %collective-permute-start.10 = (bf16[2,96,6,2,2]{1,4,3,2,0:T(2,128)(2,1)S(1)}, bf16[2,96,6,2,2]{1,4,3,2,0:T(2,128)(2,1)S(1)}, u32[]{:S(2)}, u32[]{:S(2)}) collective-permute-start(bf16[2,96,6,2,2]{1,4,3,2,0:T(2,128)(2,1)S(1)} %get-tuple-element.27), channel_id=1, source_target_pairs={{0,11},{1,10},{2,9},{3,8},{4,15},{5,14},{6,13},{7,12},{8,3},{9,2},... | collective-permute-start | bytes 27656 | tf_op jit(solution)/shard_map/ppermute | solution.py:26
  78.8 8.4 %collective-permute-start.11 = (bf16[2,96,6,2,2]{1,4,3,2,0:T(2,128)(2,1)S(1)}, bf16[2,96,6,2,2]{1,4,3,2,0:T(2,128)(2,1)S(1)}, u32[]{:S(2)}, u32[]{:S(2)}) collective-permute-start(bf16[2,96,6,2,2]{1,4,3,2,0:T(2,128)(2,1)S(1)} %get-tuple-element.26), channel_id=1, source_target_pairs={{0,12},{1,13},{2,14},{3,15},{4,8},{5,9},{6,10},{7,11},{8,4},{9,5},... | collective-permute-start | bytes 27656 | tf_op jit(solution)/shard_map/ppermute | solution.py:26
  79.7 7.5 %collective-permute-start.12 = (bf16[2,96,6,2,2]{1,4,3,2,0:T(2,128)(2,1)S(1)}, bf16[2,96,6,2,2]{1,4,3,2,0:T(2,128)(2,1)S(1)}, u32[]{:S(2)}, u32[]{:S(2)}) collective-permute-start(bf16[2,96,6,2,2]{1,4,3,2,0:T(2,128)(2,1)S(1)} %get-tuple-element.25), channel_id=1, source_target_pairs={{0,13},{1,12},{2,15},{3,14},{4,9},{5,8},{6,11},{7,10},{8,5},{9,4},... | collective-permute-start | bytes 27656 | tf_op jit(solution)/shard_map/ppermute | solution.py:26
  82.4 6.5 %collective-permute-start.13 = (bf16[2,96,6,2,2]{1,4,3,2,0:T(2,128)(2,1)S(1)}, bf16[2,96,6,2,2]{1,4,3,2,0:T(2,128)(2,1)S(1)}, u32[]{:S(2)}, u32[]{:S(2)}) collective-permute-start(bf16[2,96,6,2,2]{1,4,3,2,0:T(2,128)(2,1)S(1)} %get-tuple-element.24), channel_id=1, source_target_pairs={{0,14},{1,15},{2,12},{3,13},{4,10},{5,11},{6,8},{7,9},{8,6},{9,7},... | collective-permute-start | bytes 27656 | tf_op jit(solution)/shard_map/ppermute | solution.py:26
  83.9 5.9 %collective-permute-start.14 = (bf16[2,96,6,2,2]{1,4,3,2,0:T(2,128)(2,1)S(1)}, bf16[2,96,6,2,2]{1,4,3,2,0:T(2,128)(2,1)S(1)}, u32[]{:S(2)}, u32[]{:S(2)}) collective-permute-start(bf16[2,96,6,2,2]{1,4,3,2,0:T(2,128)(2,1)S(1)} %get-tuple-element.23), channel_id=1, source_target_pairs={{0,15},{1,14},{2,13},{3,12},{4,11},{5,10},{6,9},{7,8},{8,7},{9,6},... | collective-permute-start | bytes 27656 | tf_op jit(solution)/shard_map/ppermute | solution.py:26
